TPU v7x, 32 devices: a whole 2x2x4 slice. The times are simulated.
32 devices in a mesh: row: 4 (over y, x), col: 8 (over z, core).
Axes of the slice: x: 2, y: 2, z: 4, core: 2. Of those that a mesh axis runs over, the one named last changes fastest.
Arguments:
- root_inverse: float32 [12288, 12288], P('row', 'col'), may hold values from -6 to 6, as said below
- panel_root: float32 [2, 12288, 256], P(None, ('row', 'col')), may hold values from -0.0546875 to 0.0546875
- panel_tail: float32 [1, 256, 256], replicated, may hold values from -0.375 to 0.375
- factor_inverse: float32 [2, 256, 256], replicated, may hold values from -1 to 2, as said below
- ancestors: int32 [84], replicated, may hold values from 0 to 95, as said below
Outputs:
- border: float32 [2, 12288, 256], P(None, ('row', 'col'))
- border_tail: float32 [1, 256, 256], replicated
- diagonal: float32 [2, 256, 256], replicated
Inputs may be any that keep to these rules, and one draw needn't show every extreme that they name: `ancestors`: each of the two lists is increasing and holds distinct root blocks; the list of supernode 1 is a subset of that of supernode 0. `factor_inverse`: each block is lower triangular with a positive diagonal. `root_inverse`: the matrix is symmetric.
All inputs are finite; a program needn't handle non-finite values.
Results may differ from a plain program's by a relative error of at most 0.0001.
Values sent between devices are 32-bit elements; how exact they have to be, the bound alone decides.
No kernel may reach another device: no remote copies, remote signals or barrier semaphores. Data moves between devices by JAX's collectives and lax.ppermute only.
A program may use at most 64 MiB of HBM per device.

v0:
```python
import jax
import jax.numpy as jnp
from jax import lax
from jax.sharding import PartitionSpec as P

R = 12288
BLK = 128


def from_root(x, axis, root):
    mine = lax.axis_index(axis) == root
    return lax.psum(jnp.where(mine, x, jnp.zeros_like(x)), axis)


def product(left, right):
    return jnp.dot(left, right, precision=lax.Precision.HIGHEST, preferred_element_type=jnp.float32)


def tail_slot(later, earlier):
    return later * (later - 1) // 2 + earlier


def member(start, count, listed):
    block_ids = (start + lax.iota(jnp.int32, count)) // BLK
    return jnp.any(block_ids[:, None] == listed[None, :], axis=1).astype(jnp.float32)[:, None]


def local(root_inverse, panel_root, panel_tail, factor_inverse, ancestors):
    row_index = lax.axis_index("row")
    col_index = lax.axis_index("col")
    share = panel_root.shape[1]
    block_rows = root_inverse.shape[0]
    col_rows = root_inverse.shape[1]
    share_start = row_index * block_rows + col_index * share
    nblocks = R // BLK
    counts = [nblocks // 2, 3 * nblocks // 8]
    lists = []
    start = 0
    for node in range(2):
        lists.append(ancestors[start : start + counts[node]])
        start = start + counts[node]
    borders = []
    diagonals = []
    tails = [None]
    for node in range(2):
        listed = lists[node]
        gathered = lax.all_gather(panel_root[node : node + 1], "col", axis=1, tiled=True)
        owner = col_index * col_rows // block_rows
        offset = col_index * col_rows - owner * block_rows
        column_part = lax.dynamic_slice_in_dim(gathered, offset, col_rows, 1)
        column_part = from_root(column_part, "row", owner)
        col_start = col_index * col_rows
        joined = [column_part[0] * member(col_start, col_rows, [listed][0])][0]
        images = lax.psum_scatter(
            product(root_inverse, joined), "col", scatter_dimension=0, tiled=True
        )
        image = [images][0]
        mask = member(share_start, share, listed)
        panel = panel_root[node] * mask
        for prior in range(node):
            image = image + product(borders[prior], panel_tail[tail_slot(node, prior)])
        crossing = [product(borders[prior].T, panel) for prior in range(node)]
        carried = []
        for prior in range(node):
            value = product(diagonals[prior], panel_tail[tail_slot(node, 0)])
            carried.append(value)
        own_part = product(panel.T, image)
        base = product(factor_inverse[node].T, factor_inverse[node])
        cross = []
        joint = own_part
        for prior in range(node):
            joint = joint + product(panel_tail[tail_slot(node, prior)].T, crossing[prior])
        totals = lax.psum(tuple([joint] + crossing), ("row", "col"))
        block = base + totals[0]
        for prior in range(node):
            cross.append(totals[1 + prior] + carried[prior])
            block = block + product(panel_tail[tail_slot(node, prior)].T, carried[prior])
        for prior in range(node):
            tails[tail_slot(node, prior)] = -cross[prior]
        borders.append(-(mask * image))
        diagonals.append(block)
    return (jnp.stack(borders), jnp.stack(tails), jnp.stack(diagonals))


def solution(mesh):
    placed = (P("row", "col"), P(None, ("row", "col"), None), P(), P(), P())
    return jax.shard_map(
        local,
        mesh=mesh,
        in_specs=placed,
        out_specs=(P(None, ("row", "col"), None), P(), P()),
        check_vma=False,
    )
```

profile of v0, /device:TPU:0, one launch (start us, length us, event | category | flops | bytes accessed | tf_op | source)
XLA Modules:
  0.0 430.4 jit_solution(5512054418208885752)
XLA Ops:
  7.2 0.0 copy-start
  7.2 0.0 all-gather.3.cloned.1.call-start
  7.2 1.2 fusion.31
  8.4 0.9 copy.23
  9.3 0.0 all-gather.3.cloned.1.call-update
  9.4 0.0 all-gather.5.cloned.1.call-start
  9.4 0.9 copy.24
  10.3 0.0 all-gather.5.cloned.1.call-update
  10.4 0.0 all-reduce.7.cloned.1.call-start
  10.4 40.7 %all-gather.3.cloned.1.call-done = f32[1,3072,256]{1,2,0:T(8,128)} async-done(((f32[1,384,256]{1,2,0:T(8,128)}), f32[1,3072,256]{1,2,0:T(8,128)}) %all-gather.3.cloned.1.call-update) | async-done | bytes 3145744 | tf_op jit(solution)/shard_map/all_gather | solution.py:47
  51.1 2.7 select_bitcast_fusion.1
  53.8 36.7 %all-gather.5.cloned.1.call-done = f32[1,3072,256]{1,2,0:T(8,128)} async-done(((f32[1,384,256]{1,2,0:T(8,128)}), f32[1,3072,256]{1,2,0:T(8,128)}) %all-gather.5.cloned.1.call-update) | async-done | bytes 3145744 | tf_op jit(solution)/shard_map/all_gather | solution.py:47
  90.5 2.7 select_bitcast_fusion
  93.2 0.0 all-reduce.7.cloned.1.call-update
  93.2 0.0 reduce-scatter.3.cloned.1.call-start
  93.3 0.6 copy-done.9
  93.9 0.1 compare_reduce_fusion
  94.0 85.5 %all-reduce.7.cloned.1.call-done = (f32[1536,256]{0,1:T(8,128)}, f32[1536,256]{0,1:T(8,128)}) async-done(((f32[1536,256]{0,1:T(8,128)}, f32[1536,256]{0,1:T(8,128)}), (f32[1536,256]{0,1:T(8,128)}, f32[1536,256]{0,1:T(8,128)})) %all-reduce.7.cloned.1.call-update) | async-done | bytes 3145744 | tf_op jit(solution)/shard_map/psum | solution.py:12
  179.5 20.6 %convolution_bitcast_fusion.1 = f32[3072,256]{0,1:T(8,128)} fusion(f32[3072,1536]{1,0:T(8,128)} %param.5, f32[1536,256]{0,1:T(8,128)} %get-tuple-element.13, f32[1536]{0:T(1024)S(1)} %convert_element_type.29), kind=kOutput, calls=%fused_computation.1 | convolution fusion | flops 14495907840 | bytes 23599104 | tf_op jit(solution)/shard_map/dot_general | solution.py:16
  200.1 0.0 reduce-scatter.3.cloned.1.call-update
  200.1 0.0 reduce-scatter.5.cloned.1.call-start
  200.2 0.1 slice.24
  200.2 0.1 compare_reduce_fusion.1
  200.3 1.1 copy-done.4
  201.5 20.1 %convolution_bitcast_fusion = f32[3072,256]{0,1:T(8,128)} fusion(f32[3072,1536]{1,0:T(8,128)} %param.5, f32[1536,256]{0,1:T(8,128)S(1)} %copy-done.4, f32[1536]{0:T(1024)S(1)} %convert_element_type.31), kind=kOutput, calls=%fused_computation | convolution fusion | flops 14495907840 | bytes 23599104 | tf_op jit(solution)/shard_map/dot_general | solution.py:16
  221.6 0.0 reduce-scatter.5.cloned.1.call-update
  221.7 0.2 all-reduce.5.cloned.1.call-start
  221.9 0.1 compare_reduce_fusion.2
  222.0 0.1 compare_reduce_fusion.3
  222.1 18.5 %reduce-scatter.3.cloned.1.call-done = f32[384,256]{0,1:T(8,128)} async-done(((f32[3072,256]{0,1:T(8,128)}), f32[384,256]{0,1:T(8,128)}) %reduce-scatter.3.cloned.1.call-update) | async-done | bytes 393232 | tf_op jit(solution)/shard_map/reduce_scatter | solution.py:54
  240.6 41.8 %reduce-scatter.5.cloned.1.call-done = f32[384,256]{0,1:T(8,128)} async-done(((f32[3072,256]{0,1:T(8,128)}), f32[384,256]{0,1:T(8,128)}) %reduce-scatter.5.cloned.1.call-update) | async-done | bytes 393232 | tf_op jit(solution)/shard_map/reduce_scatter | solution.py:54
  282.5 1.8 convolution_add_fusion
  284.2 0.0 copy-start.3
  284.2 0.6 fusion.8
  284.9 0.6 fusion.9
  285.5 0.0 copy-start.5
  285.5 1.3 fusion.4
  286.8 1.3 fusion.7
  288.1 0.0 all-reduce.5.cloned.1.call-update
  288.2 0.1 pad_maximum_fusion
  288.3 1.1 copy.19
  289.5 129.3 %all-reduce.5.cloned.1.call-done = (f32[256,256]{1,0:T(8,128)}, f32[256,256]{1,0:T(8,128)}, f32[256,256]{1,0:T(8,128)}) async-done(((f32[256,256]{1,0:T(8,128)}, f32[256,256]{1,0:T(8,128)}, f32[256,256]{1,0:T(8,128)}), (f32[256,256]{1,0:T(8,128)}, f32[256,256]{1,0:T(8,128)}, f32[256,256]{1,0:T(8,128)})) %all-reduce.5.cloned.1.call-update) | async-done | bytes 786448 | tf_op jit(solution)/shard_map/psum | solution.py:73
  418.7 1.6 convolution_add_fusion.2
  420.3 0.4 fusion.15
  420.7 0.6 convolution_add_fusion.1
  421.3 0.6 fusion.3
  422.0 0.7 negate_bitcast_fusion.1
  422.7 0.8 pad_maximum_fusion.1
  (23 shorter events, 0.1 us)
Async XLA Ops:
  7.2 275.3 %copy-start = (f32[1,256,256]{2,1,0:T(8,128)S(1)}, f32[1,256,256]{2,1,0:T(8,128)}, u32[]{:S(2)}) copy-start(f32[1,256,256]{2,1,0:T(8,128)} %param.7) | copy-start | bytes 786436
  7.2 44.0 %all-gather.3.cloned.1.call-start = ((), (), s32[]{:S(2)}) async-start(), calls=%async_computation.2 | async-start | bytes 3538944 | tf_op jit(solution)/shard_map/all_gather | solution.py:47
  9.4 81.1 %all-gather.5.cloned.1.call-start = ((), (), s32[]{:S(2)}) async-start(), calls=%async_computation.4 | async-start | bytes 3538944 | tf_op jit(solution)/shard_map/all_gather | solution.py:47
  10.4 169.1 %all-reduce.7.cloned.1.call-start = ((), (), s32[]{:S(2)}) async-start(), calls=%async_computation.7 | async-start | bytes 6291456 | tf_op jit(solution)/shard_map/psum | solution.py:12
  93.2 0.7 copy-start.9
  93.2 147.4 %reduce-scatter.3.cloned.1.call-start = ((), (), s32[]{:S(2)}) async-start(), calls=%async_computation.3 | async-start | bytes 3538944 | tf_op jit(solution)/shard_map/reduce_scatter | solution.py:54
  200.1 1.4 copy-start.4
  200.1 82.4 %reduce-scatter.5.cloned.1.call-start = ((), (), s32[]{:S(2)}) async-start(), calls=%async_computation.5 | async-start | bytes 3538944 | tf_op jit(solution)/shard_map/reduce_scatter | solution.py:54
  221.6 62.6 %copy-start.1 = (f32[1,384,256]{1,2,0:T(8,128)S(1)}, f32[1,384,256]{1,2,0:T(8,128)}, u32[]{:S(2)}) copy-start(f32[1,384,256]{1,2,0:T(8,128)} %copy.24) | copy-start | bytes 1179652
  221.7 197.1 %all-reduce.5.cloned.1.call-start = ((), (), s32[]{:S(2)}) async-start(), calls=%async_computation.6 | async-start | bytes 1572864 | tf_op jit(solution)/shard_map/psum | solution.py:73
  240.6 44.2 %copy-start.2 = (f32[384,256]{0,1:T(8,128)S(1)}, f32[384,256]{0,1:T(8,128)}, u32[]{:S(2)}) copy-start(f32[384,256]{0,1:T(8,128)} %reduce-scatter.3.cloned.1.call-done) | copy-start | bytes 1179652
  284.2 2.6 copy-start.3
  285.5 2.6 copy-start.5
  288.2 130.5 %copy-start.6 = (f32[2,256,256]{2,1,0:T(8,128)S(1)}, f32[2,256,256]{2,1,0:T(8,128)}, u32[]{:S(2)}) copy-start(f32[2,256,256]{2,1,0:T(8,128)} %param.8) | copy-start | bytes 1572868
  418.7 2.0 copy-start.8
  418.7 3.2 copy-start.7
Sparse Core Ops, SparseCore 0:
  10.2 40.9 all-gather.2
  53.3 37.1 all-gather.4
  93.6 85.8 all-reduce.6
  200.2 40.3 reduce-scatter.2
  242.8 39.6 reduce-scatter.4
  288.4 130.2 all-reduce.4
where the time goes:
time: 431 us; the launch traced here: 430 us
  waiting for transfers between devices  353 us (82%)
  matrix products  49.5 us (11%)
  between operations  14.3 us (3%)
  other arithmetic  7.57 us (2%)
  local copies, waits for them, and re-layouts  5.99 us (1%)
    psum x1, waiting for transfers between devices, local(): totals = lax.psum(tuple([joint] + crossing), ('row', 'col'))  129 us
    psum x1, waiting for transfers between devices, from_root(): return lax.psum(jnp.where(mine, x, jnp.zeros_like(x)), axis)  85.5 us
    all_gather x2, waiting for transfers between devices, local(): lax.all_gather(panel_root[node:node + 1], 'col', axis=1, tiled=True)  77.4 us
    reduce_scatter x2, waiting for transfers between devices, local(): lax.psum_scatter(product(root_inverse, joined), 'col', scatter_dimension=...  60.3 us
    dot_general x11, matrix products, product(): jnp.dot(left, right, precision=lax.Precision.HIGHEST, preferred_element_t...  49.5 us
  transfers between devices with their start and end apart: 6, of which 6 were waited for; matrix products, arithmetic and copies ran while one was open for 6% of the time, Pallas kernels for 0%

commit v1 on v0

--- a/solution.py
+++ b/solution.py
@@ -5,6 +5,7 @@
 
 R = 12288
 BLK = 128
+get_the_surface = lambda row_data: lax.psum(lax.psum(row_data, axis_name="row"), axis_name="col")
 
 
 def from_root(x, axis, root):
@@ -70,7 +71,7 @@
         joint = own_part
         for prior in range(node):
             joint = joint + product(panel_tail[tail_slot(node, prior)].T, crossing[prior])
-        totals = lax.psum(tuple([joint] + crossing), ("row", "col"))
+        totals = get_the_surface(tuple([joint] + crossing))
         block = base + totals[0]
         for prior in range(node):
             cross.append(totals[1 + prior] + carried[prior])

time: 431 us -> 409 us (0.949)
  waiting for transfers between devices: 353 us -> 330 us
    psum x1 -> x2, waiting for transfers between devices: 129 us -> 107 us  [the longest x1 59.2 us: lax.psum(lax.psum(row_data, axis_name='row'), axis_name='col')]
  transfers between devices with their start and end apart: 6 -> 7, of which waited for: 6 -> 7; matrix products, arithmetic and copies ran while one was open for 6% -> 6% of each run, Pallas kernels for 0% -> 0%
where the time goes in v1:
time: 409 us; the launch traced here: 408 us
  waiting for transfers between devices  330 us (81%)
  matrix products  49.5 us (12%)
  between operations  14.3 us (3%)
  other arithmetic  7.59 us (2%)
  local copies, waits for them, and re-layouts  5.99 us (1%)
    psum x1, waiting for transfers between devices, from_root(): return lax.psum(jnp.where(mine, x, jnp.zeros_like(x)), axis)  85.5 us
    all_gather x2, waiting for transfers between devices, local(): lax.all_gather(panel_root[node:node + 1], 'col', axis=1, tiled=True)  77.3 us
    reduce_scatter x2, waiting for transfers between devices, local(): lax.psum_scatter(product(root_inverse, joined), 'col', scatter_dimension=...  60.2 us
    psum x1, waiting for transfers between devices, lax.psum(lax.psum(row_data, axis_name='row'), axis_name='col')  59.2 us
    dot_general x11, matrix products, product(): jnp.dot(left, right, precision=lax.Precision.HIGHEST, preferred_element_t...  49.5 us
    psum x1, waiting for transfers between devices, lax.psum(row_data, axis_name='row')  48.1 us
  transfers between devices with their start and end apart: 7, of which 7 were waited for; matrix products, arithmetic and copies ran while one was open for 6% of the time, Pallas kernels for 0%

profile of v1, /device:TPU:0, one launch (start us, length us, event | category | flops | bytes accessed | tf_op | source)
XLA Modules:
  0.0 408.4 jit_solution(7654089796905550173)
XLA Ops:
  7.2 0.0 all-gather.3.cloned.1.call-start
  7.2 1.2 fusion.31
  8.4 0.9 copy.23
  9.3 0.0 all-gather.3.cloned.1.call-update
  9.4 0.0 all-gather.5.cloned.1.call-start
  9.4 0.9 copy.24
  10.3 0.0 all-gather.5.cloned.1.call-update
  10.4 0.0 all-reduce.11.cloned.1.call-start
  10.4 40.7 %all-gather.3.cloned.1.call-done = f32[1,3072,256]{1,2,0:T(8,128)} async-done(((f32[1,384,256]{1,2,0:T(8,128)}), f32[1,3072,256]{1,2,0:T(8,128)}) %all-gather.3.cloned.1.call-update) | async-done | bytes 3145744 | tf_op jit(solution)/shard_map/all_gather | solution.py:48
  51.1 2.7 select_bitcast_fusion.1
  53.8 36.7 %all-gather.5.cloned.1.call-done = f32[1,3072,256]{1,2,0:T(8,128)} async-done(((f32[1,384,256]{1,2,0:T(8,128)}), f32[1,3072,256]{1,2,0:T(8,128)}) %all-gather.5.cloned.1.call-update) | async-done | bytes 3145744 | tf_op jit(solution)/shard_map/all_gather | solution.py:48
  90.5 2.8 select_bitcast_fusion
  93.2 0.0 all-reduce.11.cloned.1.call-update
  93.2 0.0 reduce-scatter.3.cloned.1.call-start
  93.3 0.6 copy-done.9
  93.9 0.1 compare_reduce_fusion
  94.0 85.5 %all-reduce.11.cloned.1.call-done = (f32[1536,256]{0,1:T(8,128)}, f32[1536,256]{0,1:T(8,128)}) async-done(((f32[1536,256]{0,1:T(8,128)}, f32[1536,256]{0,1:T(8,128)}), (f32[1536,256]{0,1:T(8,128)}, f32[1536,256]{0,1:T(8,128)})) %all-reduce.11.cloned.1.call-update) | async-done | bytes 3145744 | tf_op jit(solution)/shard_map/psum | solution.py:13
  179.5 20.6 %convolution_bitcast_fusion.1 = f32[3072,256]{0,1:T(8,128)} fusion(f32[3072,1536]{1,0:T(8,128)} %param.5, f32[1536,256]{0,1:T(8,128)} %get-tuple-element.16, f32[1536]{0:T(1024)S(1)} %convert_element_type.29), kind=kOutput, calls=%fused_computation.1 | convolution fusion | flops 14495907840 | bytes 23599104 | tf_op jit(solution)/shard_map/dot_general | solution.py:17
  200.1 0.0 reduce-scatter.3.cloned.1.call-update
  200.1 0.0 reduce-scatter.5.cloned.1.call-start
  200.1 0.1 slice.24
  200.2 0.1 compare_reduce_fusion.1
  200.3 1.1 copy-done.4
  201.5 20.1 %convolution_bitcast_fusion = f32[3072,256]{0,1:T(8,128)} fusion(f32[3072,1536]{1,0:T(8,128)} %param.5, f32[1536,256]{0,1:T(8,128)S(1)} %copy-done.4, f32[1536]{0:T(1024)S(1)} %convert_element_type.31), kind=kOutput, calls=%fused_computation | convolution fusion | flops 14495907840 | bytes 23599104 | tf_op jit(solution)/shard_map/dot_general | solution.py:17
  221.6 0.0 reduce-scatter.5.cloned.1.call-update
  221.6 0.2 all-reduce.9.cloned.1.call-start
  221.9 0.1 compare_reduce_fusion.2
  222.0 0.1 compare_reduce_fusion.3
  222.1 18.5 %reduce-scatter.3.cloned.1.call-done = f32[384,256]{0,1:T(8,128)} async-done(((f32[3072,256]{0,1:T(8,128)}), f32[384,256]{0,1:T(8,128)}) %reduce-scatter.3.cloned.1.call-update) | async-done | bytes 393232 | tf_op jit(solution)/shard_map/reduce_scatter | solution.py:55
  240.6 41.7 %reduce-scatter.5.cloned.1.call-done = f32[384,256]{0,1:T(8,128)} async-done(((f32[3072,256]{0,1:T(8,128)}), f32[384,256]{0,1:T(8,128)}) %reduce-scatter.5.cloned.1.call-update) | async-done | bytes 393232 | tf_op jit(solution)/shard_map/reduce_scatter | solution.py:55
  282.3 1.8 convolution_add_fusion
  284.1 0.6 fusion.8
  284.8 0.6 fusion.9
  285.4 1.3 fusion.4
  286.7 1.3 fusion.7
  288.0 0.0 all-reduce.9.cloned.1.call-update
  288.0 0.0 all-reduce.7.cloned.1.call-start
  288.1 48.1 %all-reduce.9.cloned.1.call-done = (f32[256,256]{1,0:T(8,128)}, f32[256,256]{1,0:T(8,128)}, f32[256,256]{1,0:T(8,128)}) async-done(((f32[256,256]{1,0:T(8,128)}, f32[256,256]{1,0:T(8,128)}, f32[256,256]{1,0:T(8,128)}), (f32[256,256]{1,0:T(8,128)}, f32[256,256]{1,0:T(8,128)}, f32[256,256]{1,0:T(8,128)})) %all-reduce.9.cloned.1.call-update) | async-done | bytes 786448 | tf_op jit(solution)/shard_map/psum | solution.py:8
  336.2 0.0 all-reduce.7.cloned.1.call-update
  336.4 0.1 pad_maximum_fusion
  336.4 1.1 copy.19
  337.6 59.2 %all-reduce.7.cloned.1.call-done = (f32[256,256]{1,0:T(8,128)}, f32[256,256]{1,0:T(8,128)}, f32[256,256]{1,0:T(8,128)}) async-done(((f32[256,256]{1,0:T(8,128)}, f32[256,256]{1,0:T(8,128)}, f32[256,256]{1,0:T(8,128)}), (f32[256,256]{1,0:T(8,128)}, f32[256,256]{1,0:T(8,128)}, f32[256,256]{1,0:T(8,128)})) %all-reduce.7.cloned.1.call-update) | async-done | bytes 786448 | tf_op jit(solution)/shard_map/psum | solution.py:8
  396.8 1.6 convolution_add_fusion.2
  398.4 0.4 fusion.15
  398.8 0.6 convolution_add_fusion.1
  399.4 0.6 fusion.3
  400.0 0.7 negate_bitcast_fusion.1
  400.7 0.8 pad_maximum_fusion.1
  (26 shorter events, 0.2 us)
Async XLA Ops:
  7.2 275.2 %copy-start = (f32[1,256,256]{2,1,0:T(8,128)S(1)}, f32[1,256,256]{2,1,0:T(8,128)}, u32[]{:S(2)}) copy-start(f32[1,256,256]{2,1,0:T(8,128)} %param.7) | copy-start | bytes 786436
  7.2 44.0 %all-gather.3.cloned.1.call-start = ((), (), s32[]{:S(2)}) async-start(), calls=%async_computation.2 | async-start | bytes 3538944 | tf_op jit(solution)/shard_map/all_gather | solution.py:48
  9.4 81.1 %all-gather.5.cloned.1.call-start = ((), (), s32[]{:S(2)}) async-start(), calls=%async_computation.4 | async-start | bytes 3538944 | tf_op jit(solution)/shard_map/all_gather | solution.py:48
  10.4 169.1 %all-reduce.11.cloned.1.call-start = ((), (), s32[]{:S(2)}) async-start(), calls=%async_computation.8 | async-start | bytes 6291456 | tf_op jit(solution)/shard_map/psum | solution.py:13
  93.2 0.7 copy-start.9
  93.2 147.4 %reduce-scatter.3.cloned.1.call-start = ((), (), s32[]{:S(2)}) async-start(), calls=%async_computation.3 | async-start | bytes 3538944 | tf_op jit(solution)/shard_map/reduce_scatter | solution.py:55
  200.1 1.4 copy-start.4
  200.1 82.2 %reduce-scatter.5.cloned.1.call-start = ((), (), s32[]{:S(2)}) async-start(), calls=%async_computation.5 | async-start | bytes 3538944 | tf_op jit(solution)/shard_map/reduce_scatter | solution.py:55
  221.6 62.5 %copy-start.1 = (f32[1,384,256]{1,2,0:T(8,128)S(1)}, f32[1,384,256]{1,2,0:T(8,128)}, u32[]{:S(2)}) copy-start(f32[1,384,256]{1,2,0:T(8,128)} %copy.24) | copy-start | bytes 1179652
  221.6 114.6 %all-reduce.9.cloned.1.call-start = ((), (), s32[]{:S(2)}) async-start(), calls=%async_computation.7 | async-start | bytes 1572864 | tf_op jit(solution)/shard_map/psum | solution.py:8
  240.6 44.1 %copy-start.2 = (f32[384,256]{0,1:T(8,128)S(1)}, f32[384,256]{0,1:T(8,128)}, u32[]{:S(2)}) copy-start(f32[384,256]{0,1:T(8,128)} %reduce-scatter.3.cloned.1.call-done) | copy-start | bytes 1179652
  284.1 2.6 copy-start.3
  285.4 2.6 copy-start.5
  288.0 108.7 %all-reduce.7.cloned.1.call-start = ((), (), s32[]{:S(2)}) async-start(), calls=%async_computation.6 | async-start | bytes 1572864 | tf_op jit(solution)/shard_map/psum | solution.py:8
  336.3 60.4 %copy-start.6 = (f32[2,256,256]{2,1,0:T(8,128)S(1)}, f32[2,256,256]{2,1,0:T(8,128)}, u32[]{:S(2)}) copy-start(f32[2,256,256]{2,1,0:T(8,128)} %param.8) | copy-start | bytes 1572868
  396.8 2.0 copy-start.8
  396.8 3.2 copy-start.7
Sparse Core Ops, SparseCore 0:
  10.2 40.9 all-gather.2
  53.3 37.1 all-gather.4
  93.6 85.8 all-reduce.10
  200.2 40.3 reduce-scatter.2
  242.8 39.5 reduce-scatter.4
  288.2 48.0 all-reduce.8
  338.8 57.9 all-reduce.6
